TPU v7x, 128 devices: a whole 4x4x4 slice. The times are simulated.
128 devices in a mesh: dp: 16 (over y, x), seq: 8 (over z, core).
Axes of the slice: x: 4, y: 4, z: 4, core: 2. Of those that a mesh axis runs over, the one named last changes fastest.
Arguments:
- feats: bfloat16 [65536, 1024], P(('dp', 'seq')), may hold values from -6 to 6
- gain: float32 [1024], replicated, may hold values from 0.1 to 1.9
- w_qkv: bfloat16 [1024, 3072], replicated, as said below
- w_out: bfloat16 [1024, 1024], replicated, may hold values from -3 to 3
- block_cols: int32 [16, 32, 8], P('dp'), may hold values from 0 to 31, as said below
- block_counts: int32 [16, 32], P('dp'), may hold values from 1 to 8, 128 in all within a row
- cotan: bfloat16 [65536, 1024], P(('dp', 'seq')), may hold values from -0.3984375 to 0.3984375
Outputs:
- result: bfloat16 [65536, 1024], P(('dp', 'seq'))
- grad_feats: bfloat16 [65536, 1024], P(('dp', 'seq'))
- grad_qkv: bfloat16 [1024, 3072], P('seq')
- grad_out: bfloat16 [1024, 1024], P('seq')
Inputs may be any that keep to these rules, and one draw needn't show every extreme that they name: `block_cols`: for every batch and row block r, the 8 listed column blocks are distinct and the first is r itself. `block_counts`: each batch's counts sum to 128. `w_qkv`: entries lie within 70 / sqrt(1024) in magnitude.
All inputs are finite; a program needn't handle non-finite values.
Results may differ from a plain program's by a relative error of at most 0.014.
Values may be sent and summed in bfloat16 or wider, within the bound.
A program may use at most 128 MiB of HBM per device.

v0:
```python
import jax
import jax.numpy as jnp
from jax import lax
from jax.sharding import PartitionSpec as P

HD = 64
BLK = 128
MAXB = 8
EPSILON = 1e-05


def layer_norm(feats, gain):
    values_f = feats.astype(jnp.float32)
    centred = values_f - jnp.mean(values_f, axis=1, keepdims=True)
    inverse = lax.rsqrt(jnp.mean(centred * centred, axis=1, keepdims=True) + EPSILON)
    scaled = centred * inverse
    return (scaled, inverse, (scaled * gain[None, :]).astype(jnp.bfloat16))


def live_slots(counts):
    return jnp.arange(MAXB, dtype=jnp.int32)[None, :] < counts[:, None]


def contract_rows(left_cols, right_cols):
    return lax.dot_general(
        left_cols, right_cols, (((0,), (0,)), ((), ())), preferred_element_type=jnp.float32
    )


def stacked_table(key_heads, value_heads, block_total, head_count):
    key_b = key_heads.reshape(block_total, BLK, head_count, HD)
    value_b = value_heads.reshape(block_total, BLK, head_count, HD)
    return jnp.concatenate([key_b, value_b], axis=3).reshape(block_total, BLK * head_count * 2 * HD)


def select_blocks(onehot, table, head_count):
    picked = jnp.einsum("gsc,cf->gsf", onehot, table, preferred_element_type=jnp.float32).astype(
        jnp.bfloat16
    )
    picked = picked.reshape(onehot.shape[0], onehot.shape[1], BLK, head_count, 2 * HD)
    return (picked[..., :HD], picked[..., HD:])


def forward_blocks(query_heads, key_heads, value_heads, col_blocks, counts, head_count):
    per_step = 4
    block_total = query_heads.shape[0] // BLK
    steps_count = block_total // per_step
    query_b = query_heads.reshape(steps_count, per_step, BLK, head_count, HD)
    table = stacked_table(key_heads, value_heads, block_total, head_count)
    col_steps = col_blocks.reshape(steps_count, per_step, MAXB)
    count_steps = counts.reshape(steps_count, per_step)
    block_range = jnp.arange(block_total, dtype=jnp.int32)
    score_scale = HD ** (-0.5)

    def forward_block_step(inputs):
        query_g, col_g, count_g = inputs
        onehot = (col_g[:, :, None] == block_range[None, None, :]).astype(jnp.bfloat16)
        key_g, value_g = select_blocks(onehot, table, head_count)
        scores = (
            jnp.einsum("gqhd,gskhd->ghqsk", query_g, key_g, preferred_element_type=jnp.float32)
            * score_scale
        )
        live_mask = live_slots(count_g)[:, None, None, :, None]
        row_max = jnp.max(jnp.where(live_mask, scores, -jnp.inf), axis=(3, 4), keepdims=True)
        row_total = jnp.sum(
            jnp.where(live_mask, jnp.exp(scores - row_max), 0.0), axis=(3, 4), keepdims=True
        )
        log_total = row_max + jnp.log(row_total)
        probabilities = jnp.where(live_mask, jnp.exp(scores - log_total), 0.0).astype(jnp.bfloat16)
        attended = jnp.einsum(
            "ghqsk,gskhd->gqhd", probabilities, value_g, preferred_element_type=jnp.float32
        )
        return (attended.astype(jnp.bfloat16), log_total[:, :, :, 0, 0])

    attended, log_total = lax.map(forward_block_step, (query_b, col_steps, count_steps))
    return (attended.reshape(query_heads.shape), log_total)


def backward_blocks(
    query_heads,
    key_heads,
    value_heads,
    attended_heads,
    grad_heads,
    log_total,
    col_blocks,
    counts,
    head_count,
):
    per_step = 4
    block_total = query_heads.shape[0] // BLK
    steps_count = block_total // per_step
    query_b = query_heads.reshape(steps_count, per_step, BLK, head_count, HD)
    grad_b = grad_heads.reshape(steps_count, per_step, BLK, head_count, HD)
    attended_b = attended_heads.reshape(steps_count, per_step, BLK, head_count, HD)
    table = stacked_table(key_heads, value_heads, block_total, head_count)
    col_steps = col_blocks.reshape(steps_count, per_step, MAXB)
    count_steps = counts.reshape(steps_count, per_step)
    delta_all = jnp.sum(attended_b.astype(jnp.float32) * grad_b.astype(jnp.float32), axis=4)
    block_range = jnp.arange(block_total, dtype=jnp.int32)
    score_scale = HD ** (-0.5)

    def backward_block_step(carry, inputs):
        key_sum, value_sum = carry
        query_g, grad_g, delta_g, log_g, col_g, count_g = inputs
        matches = col_g[:, :, None] == block_range[None, None, :]
        key_g, value_g = select_blocks(matches.astype(jnp.bfloat16), table, head_count)
        scores = (
            jnp.einsum("gqhd,gskhd->ghqsk", query_g, key_g, preferred_element_type=jnp.float32)
            * score_scale
        )
        live_mask = live_slots(count_g)[:, None, None, :, None]
        probabilities = jnp.where(
            live_mask, jnp.exp(scores - log_g[:, :, :, None, None]), 0.0
        ).astype(jnp.bfloat16)
        prob_grad = jnp.einsum(
            "gqhd,gskhd->ghqsk", grad_g, value_g, preferred_element_type=jnp.float32
        )
        delta_t = jnp.transpose(delta_g, (0, 2, 1))[:, :, :, None, None]
        score_grad = (
            probabilities.astype(jnp.float32) * (prob_grad - delta_t) * score_scale
        ).astype(jnp.bfloat16)
        query_grad = jnp.einsum(
            "ghqsk,gskhd->gqhd", score_grad, key_g, preferred_element_type=jnp.float32
        ).astype(jnp.bfloat16)
        key_pairs = jnp.einsum(
            "ghqsk,gqhd->gskhd", score_grad, query_g, preferred_element_type=jnp.float32
        )
        value_pairs = jnp.einsum(
            "ghqsk,gqhd->gskhd", probabilities, grad_g, preferred_element_type=jnp.float32
        )
        selector = matches.astype(jnp.float32)
        key_sum = key_sum + jnp.einsum(
            "gsc,gskhd->ckhd", selector, key_pairs, precision=lax.Precision.HIGHEST
        )
        value_sum = value_sum + jnp.einsum(
            "gsc,gskhd->ckhd", selector, value_pairs, precision=lax.Precision.HIGHEST
        )
        return ((key_sum, value_sum), query_grad)

    zeros_f = jnp.zeros((block_total, BLK, head_count, HD), jnp.float32)
    (key_sum, value_sum), query_grad = lax.scan(
        backward_block_step,
        (zeros_f, zeros_f),
        (query_b, grad_b, delta_all, log_total, col_steps, count_steps),
    )
    shape = query_heads.shape
    return (
        query_grad.reshape(shape),
        key_sum.reshape(shape).astype(jnp.bfloat16),
        value_sum.reshape(shape).astype(jnp.bfloat16),
    )


def body(feats, gain, w_qkv, w_out, block_cols, block_counts, cotan):
    seq_count = lax.axis_size("seq")
    model_width = feats.shape[1]
    qkv_width = 3 * model_width
    scaled, inverse, normed = layer_norm(feats, gain)
    mixed_proj = jnp.dot(normed, w_qkv, preferred_element_type=jnp.float32).astype(jnp.bfloat16)
    query_rows = mixed_proj[:, :model_width]
    key_rows = mixed_proj[:, model_width : 2 * model_width]
    value_rows = mixed_proj[:, 2 * model_width :]
    query_heads, key_heads, value_heads = (
        lax.all_to_all(query_rows, "seq", split_axis=1, concat_axis=0, tiled=True),
        lax.all_to_all(key_rows, "seq", split_axis=1, concat_axis=0, tiled=True),
        lax.all_to_all(value_rows, "seq", split_axis=1, concat_axis=0, tiled=True),
    )
    head_count = query_heads.shape[1] // HD
    col_blocks = block_cols[0]
    counts = block_counts[0]
    attended_heads, log_total = forward_blocks(
        query_heads, key_heads, value_heads, col_blocks, counts, head_count
    )
    attended = lax.all_to_all(attended_heads, "seq", split_axis=0, concat_axis=1, tiled=True)
    result = (
        feats.astype(jnp.float32) + jnp.dot(attended, w_out, preferred_element_type=jnp.float32)
    ).astype(jnp.bfloat16)
    grad_att = lax.dot_general(
        cotan, w_out, (((1,), (1,)), ((), ())), preferred_element_type=jnp.float32
    ).astype(jnp.bfloat16)
    grad_heads = lax.all_to_all(grad_att, "seq", split_axis=1, concat_axis=0, tiled=True)
    query_grad, key_grad, value_grad = backward_blocks(
        query_heads,
        key_heads,
        value_heads,
        attended_heads,
        grad_heads,
        log_total,
        col_blocks,
        counts,
        head_count,
    )
    query_back, key_back, value_back = (
        lax.all_to_all(query_grad, "seq", split_axis=0, concat_axis=1, tiled=True),
        lax.all_to_all(key_grad, "seq", split_axis=0, concat_axis=1, tiled=True),
        lax.all_to_all(value_grad, "seq", split_axis=0, concat_axis=1, tiled=True),
    )
    grad_mixed = jnp.concatenate([query_back, key_back, value_back], axis=1)
    grad_normed = lax.dot_general(
        grad_mixed, w_qkv, (((1,), (1,)), ((), ())), preferred_element_type=jnp.float32
    )
    gained = grad_normed * gain[None, :]
    mean_one = jnp.mean(gained, axis=1, keepdims=True)
    mean_two = jnp.mean(gained * scaled, axis=1, keepdims=True)
    grad_feats = (
        cotan.astype(jnp.float32) + inverse * (gained - mean_one - scaled * mean_two)
    ).astype(jnp.bfloat16)
    summed = lax.psum(
        jnp.concatenate(
            [contract_rows(normed, grad_mixed), contract_rows(attended, cotan)], axis=1
        ),
        ("dp", "seq"),
    )
    shard_rows = model_width // seq_count
    own_rows = lax.dynamic_slice_in_dim(summed, lax.axis_index("seq") * shard_rows, shard_rows, 0)
    grad_qkv = own_rows[:, :qkv_width].astype(jnp.bfloat16)
    grad_out = own_rows[:, qkv_width:].astype(jnp.bfloat16)
    return (result, grad_feats, grad_qkv, grad_out)


def solution(mesh):
    in_specs = (
        P(("dp", "seq"), None),
        P(),
        P(),
        P(),
        P("dp", None, None),
        P("dp", None),
        P(("dp", "seq"), None),
    )
    out_specs = (P(("dp", "seq"), None), P(("dp", "seq"), None), P("seq", None), P("seq", None))
    return jax.shard_map(body, mesh=mesh, in_specs=in_specs, out_specs=out_specs, check_vma=False)
```

profile of v0, /device:TPU:0, one launch (start us, length us, event | category | flops | bytes accessed | tf_op | source)
XLA Modules:
  0.0 628.2 jit_solution(8621975070728321357)
XLA Ops:
  4.0 6.7 %convolution_convert_fusion.2 = bf16[512,3072]{1,0:T(8,128)(2,1)S(1)} fusion(bf16[1024,3072]{1,0:T(8,128)(2,1)} %param.13, bf16[512,1024]{1,0:T(8,128)(2,1)S(1)} %copy-done.8, f32[1024]{0:T(1024)S(1)} %copy-done.19, f32[512]{0:T(512)S(1)} %add_rsqrt_fusion, f32[512]{0:T(512)S(1)} %broadcast_multiply_fusion.2), kind=kOutput, calls=%fused_computation.70 | convolution fusion | flops 3225419776 | bytes 10493952 | tf_op jit(solution)/shard_map/dot_general | solution.py:160
  13.7 5.4 all-to-all-start.1
  21.4 13.7 %all-to-all-done.1 = bf16[512,8,128]{0,2,1:T(8,128)(2,1)S(1)} async-done(((bf16[512,8,128]{0,2,1:T(8,128)(2,1)}), bf16[512,8,128]{0,2,1:T(8,128)(2,1)S(1)}, u32[]{:S(2)}, u32[]{:S(2)}) %all-to-all-start.1) | async-done | bytes 1048608 | tf_op jit(solution)/shard_map/all_to_all | solution.py:167
  35.0 4.2 all-to-all-start
  41.6 13.7 %all-to-all-done = bf16[512,8,128]{0,2,1:T(8,128)(2,1)} async-done(((bf16[512,8,128]{0,2,1:T(8,128)(2,1)}), bf16[512,8,128]{0,2,1:T(8,128)(2,1)}, u32[]{:S(2)}, u32[]{:S(2)}) %all-to-all-start) | async-done | bytes 1048608 | tf_op jit(solution)/shard_map/all_to_all | solution.py:166
  55.2 4.2 all-to-all-start.2
  77.0 4.7 copy.69
  81.7 4.5 reshape.177
  86.2 5.2 all-to-all-start.4
  94.5 59.6 %while.28 = (s32[]{:T(128)}, bf16[8,4,128,2,64]{2,1,4,3,0:T(4,128)(2,1)S(1)}, f32[8,4,2,128]{3,2,1,0:T(2,128)S(1)}, s32[8,4,8]{2,1,0:T(4,128)S(1)}, bf16[32,3276...) while((s32[]{:T(128)}, ...), condition=%wide.region_5.6_spmd.clone, body=%wide.region_2.5_spmd.clone.sunk | while | flops 348192800 | bytes 23626400 | solution.py:75
  155.3 4.8 all-to-all-start.3
  165.6 239.2 %while.29 = (s32[]{:T(128)}, f32[32,128,2,64]{1,0,3,2:T(8,128)}, f32[32,128,2,64]{1,0,3,2:T(8,128)}, bf16[8,4,128,2,64]{2,1,4,3,0:T(4,128)(2,1)}, s32[8,4,8]{2,1...) while((s32[]{:T(128)}, f32[32,128,2,64]{1,0,3,2:T(8,128)}, ...), condition=%wide.region_8.9_spmd.clone, body=%wide.region_7.8_spmd.clone.sunk | while | flops 1153502208 | bytes 98731120 | solution.py:142
  182.9 5.5 bitcast_add_fusion.4
  189.9 3.5 bitcast_add_fusion.5
  212.2 6.1 bitcast_add_fusion.4
  242.1 6.1 bitcast_add_fusion.4
  272.0 6.1 bitcast_add_fusion.4
  302.0 6.1 bitcast_add_fusion.4
  331.9 6.1 bitcast_add_fusion.4
  361.8 6.1 bitcast_add_fusion.4
  391.8 6.1 bitcast_add_fusion.4
  410.6 4.8 all-to-all-start.7
  421.3 10.2 %all-to-all-done.7 = bf16[8,512,128]{1,2,0:T(8,128)(2,1)} async-done(((bf16[8,512,128]{1,2,0:T(8,128)(2,1)}), bf16[8,512,128]{1,2,0:T(8,128)(2,1)}, u32[]{:S(2)}, u32[]{:S(2)}) %all-to-all-start.7) | async-done | bytes 1048608 | tf_op jit(solution)/shard_map/all_to_all | solution.py:197
  431.5 4.2 all-to-all-start.6
  437.0 14.7 %all-to-all-done.6 = bf16[8,512,128]{1,2,0:T(8,128)(2,1)} async-done(((bf16[8,512,128]{1,2,0:T(8,128)(2,1)}), bf16[8,512,128]{1,2,0:T(8,128)(2,1)}, u32[]{:S(2)}, u32[]{:S(2)}) %all-to-all-start.6) | async-done | bytes 1048608 | tf_op jit(solution)/shard_map/all_to_all | solution.py:196
  451.7 4.2 all-to-all-start.5
  456.0 4.8 fusion.76
  464.3 7.6 %all-to-all-done.5 = bf16[8,512,128]{1,2,0:T(8,128)(2,1)} async-done(((bf16[8,512,128]{1,2,0:T(8,128)(2,1)}), bf16[8,512,128]{1,2,0:T(8,128)(2,1)}, u32[]{:S(2)}, u32[]{:S(2)}) %all-to-all-start.5) | async-done | bytes 1048608 | tf_op jit(solution)/shard_map/all_to_all | solution.py:195
  471.9 8.9 %multiply_reduce_fusion.1 = (f32[512]{0:T(512)S(1)}, f32[512]{0:T(512)S(1)}, f32[512,1024]{1,0:T(8,128)}) fusion(f32[1024]{0:T(1024)S(1)} %copy-done.20, f32[512]{0:T(512)S(1)} %copy-done.17, f32[512]{0:T(512)S(1)} %copy-done.15, bf16[512,1024]{1,0:T(8,128)(2,1)S(1)} %copy-done.9, bf16[1024,3072]{1,0:T(8,128)(2,1)} %param.13, ...), kind=kOutput, calls=%fused_computation.91 | convolution fusion | flops 3234331648 | bytes 12595200 | tf_op jit(solution)/shard_map/dot_general | solution.py:200
  480.8 5.8 fusion.67
  486.6 6.0 pad_maximum_fusion
  492.7 130.1 %all-reduce.1 = bf16[1024,4096]{1,0:T(8,128)(2,1)} all-reduce(f32[1024,4096]{1,0:T(8,128)} %pad_maximum_fusion), channel_id=1, replica_groups=mesh['dp'=16,'seq'=8] {'dp','seq'}, use_global_device_ids=true, to_apply=%region_11.12 | all-reduce | flops 4194304 | bytes 25165824 | tf_op jit(solution)/shard_map/psum | solution.py:209
  (402 shorter events, 304.6 us)
Async XLA Ops:
  0.6 60.2 %copy-start = (bf16[1024,1024]{1,0:T(8,128)(2,1)S(1)}, bf16[1024,1024]{1,0:T(8,128)(2,1)}, u32[]{:S(2)}) copy-start(bf16[1024,1024]{1,0:T(8,128)(2,1)} %param.14) | copy-start | bytes 6291460
  2.3 8.4 %copy-start.14 = (f32[512]{0:T(512)}, f32[512]{0:T(512)S(1)}, u32[]{:S(2)}) copy-start(f32[512]{0:T(512)S(1)} %broadcast_multiply_fusion.2) | copy-start | bytes 6148
  3.9 6.7 %copy-start.16 = (f32[512]{0:T(512)}, f32[512]{0:T(512)S(1)}, u32[]{:S(2)}) copy-start(f32[512]{0:T(512)S(1)} %add_rsqrt_fusion) | copy-start | bytes 6148
  13.7 21.4 %all-to-all-start.1 = ((bf16[512,8,128]{0,2,1:T(8,128)(2,1)}), bf16[512,8,128]{0,2,1:T(8,128)(2,1)S(1)}, u32[]{:S(2)}, u32[]{:S(2)}) async-start(bf16[512,8,128]{0,2,1:T(8,128)(2,1)} %bitcast.208), calls=%async_computation.1 | async-start | bytes 2097152 | tf_op jit(solution)/shard_map/all_to_all | solution.py:167
  35.0 20.2 %all-to-all-start = ((bf16[512,8,128]{0,2,1:T(8,128)(2,1)}), bf16[512,8,128]{0,2,1:T(8,128)(2,1)}, u32[]{:S(2)}, u32[]{:S(2)}) async-start(bf16[512,8,128]{0,2,1:T(8,128)(2,1)} %bitcast.207), calls=%async_computation | async-start | bytes 2097152 | tf_op jit(solution)/shard_map/all_to_all | solution.py:166
  39.3 20.2 %copy-start.18 = (s32[1,32,8]{1,2,0:T(8,128)S(1)}, s32[1,32,8]{1,2,0:T(8,128)}, u32[]{:S(2)}) copy-start(s32[1,32,8]{1,2,0:T(8,128)} %param.15) | copy-start | bytes 3076
  39.3 20.8 %copy-start.21 = (s32[1,32]{1,0:T(1,128)S(1)}, s32[1,32]{1,0:T(1,128)}, u32[]{:S(2)}) copy-start(s32[1,32]{1,0:T(1,128)} %param.16) | copy-start | bytes 388
  55.2 31.0 %all-to-all-start.2 = ((bf16[512,8,128]{0,2,1:T(8,128)(2,1)}), bf16[512,8,128]{0,2,1:T(8,128)(2,1)}, u32[]{:S(2)}, u32[]{:S(2)}) async-start(bf16[512,8,128]{0,2,1:T(8,128)(2,1)} %bitcast.206), calls=%async_computation.2 | async-start | bytes 2097152 | tf_op jit(solution)/shard_map/all_to_all | solution.py:165
  86.2 69.1 %all-to-all-start.4 = ((bf16[512,8,128]{0,2,1:T(8,128)(2,1)}), bf16[512,8,128]{0,2,1:T(8,128)(2,1)}, u32[]{:S(2)}, u32[]{:S(2)}) async-start(bf16[512,8,128]{0,2,1:T(8,128)(2,1)} %bitcast.9), calls=%async_computation.4 | async-start | bytes 2097152 | tf_op jit(solution)/shard_map/all_to_all | solution.py:182
  155.3 255.3 %all-to-all-start.3 = ((bf16[8,512,128]{1,2,0:T(8,128)(2,1)}), bf16[8,512,128]{1,2,0:T(8,128)(2,1)}, u32[]{:S(2)}, u32[]{:S(2)}) async-start(bf16[8,512,128]{1,2,0:T(8,128)(2,1)} %all_to_all.109), calls=%async_computation.3 | async-start | bytes 2097152 | tf_op jit(solution)/shard_map/all_to_all | solution.py:175
  182.9 5.5 copy-start.4
  189.9 3.5 copy-start.2
  212.2 6.1 copy-start.4
  219.9 3.5 copy-start.2
  242.1 6.1 copy-start.4
  249.8 3.5 copy-start.2
  272.0 6.1 copy-start.4
  279.7 3.5 copy-start.2
  302.0 6.1 copy-start.4
  309.7 3.5 copy-start.2
  331.9 6.1 copy-start.4
  361.8 6.1 copy-start.4
  391.8 6.1 copy-start.4
  410.6 20.9 %all-to-all-start.7 = ((bf16[8,512,128]{1,2,0:T(8,128)(2,1)}), bf16[8,512,128]{1,2,0:T(8,128)(2,1)}, u32[]{:S(2)}, u32[]{:S(2)}) async-start(bf16[8,512,128]{1,2,0:T(8,128)(2,1)} %copy.80), calls=%async_computation.7 | async-start | bytes 2097152 | tf_op jit(solution)/shard_map/all_to_all | solution.py:197
  418.7 17.1 %copy-start.10 = (bf16[8,4,128,2,64]{2,1,4,3,0:T(4,128)(2,1)S(1)}, bf16[8,4,128,2,64]{2,1,4,3,0:T(4,128)(2,1)}, u32[]{:S(2)}) copy-start(bf16[8,4,128,2,64]{2,1,4,3,0:T(4,128)(2,1)} %get-tuple-element.113) | copy-start | bytes 3145732
  431.5 20.2 %all-to-all-start.6 = ((bf16[8,512,128]{1,2,0:T(8,128)(2,1)}), bf16[8,512,128]{1,2,0:T(8,128)(2,1)}, u32[]{:S(2)}, u32[]{:S(2)}) async-start(bf16[8,512,128]{1,2,0:T(8,128)(2,1)} %copy.79), calls=%async_computation.6 | async-start | bytes 2097152 | tf_op jit(solution)/shard_map/all_to_all | solution.py:196
  451.7 20.2 %all-to-all-start.5 = ((bf16[8,512,128]{1,2,0:T(8,128)(2,1)}), bf16[8,512,128]{1,2,0:T(8,128)(2,1)}, u32[]{:S(2)}, u32[]{:S(2)}) async-start(bf16[8,512,128]{1,2,0:T(8,128)(2,1)} %all_to_all.116), calls=%async_computation.5 | async-start | bytes 2097152 | tf_op jit(solution)/shard_map/all_to_all | solution.py:195
  456.0 4.8 copy-start.9
  460.8 11.1 %copy-start.15 = (f32[512]{0:T(512)S(1)}, f32[512]{0:T(512)}, u32[]{:S(2)}) copy-start(f32[512]{0:T(512)} %copy-done.14) | copy-start | bytes 6148
  460.8 11.1 %copy-start.17 = (f32[512]{0:T(512)S(1)}, f32[512]{0:T(512)}, u32[]{:S(2)}) copy-start(f32[512]{0:T(512)} %copy-done.16) | copy-start | bytes 6148
  460.8 11.1 %copy-start.20 = (f32[1024]{0:T(1024)S(1)}, f32[1024]{0:T(1024)}, u32[]{:S(2)}) copy-start(f32[1024]{0:T(1024)} %param.12) | copy-start | bytes 12292
  480.8 5.8 copy-start.11
  (47 other events, 107.5 us)
where the time goes:
time: 637 us; the launch traced here: 628 us
  matrix products  231 us (36%)
  local copies, waits for them, and re-layouts  138 us (22%)
  blocking collectives  130 us (20%)
  waiting for transfers between devices  59.9 us (9%)
  starting transfers between devices  37.2 us (6%)
  other arithmetic  28.9 us (5%)
    psum x1, blocking collectives, body(): lax.psum(jnp.concatenate([contract_rows(normed, grad_mixed), contract_row...  130 us
    dot_general x8, matrix products, backward_block_step(): jnp.einsum('gsc,gskhd->ckhd', selector, key_pairs, precision=lax.Precisio...  48.1 us
    while x120, local copies, waits for them, and re-layouts  42.8 us
    dot_general x16, matrix products, select_blocks(): jnp.einsum('gsc,cf->gsf', onehot, table, preferred_element_type=jnp.float32)  37.4 us
    slice x16, local copies, waits for them, and re-layouts, select_blocks(): return (picked[..., :HD], picked[..., HD:])  31.4 us
    dot_general x8, matrix products, backward_block_step(): jnp.einsum('gsc,gskhd->ckhd', selector, value_pairs, precision=lax.Precis...  28.1 us
    dot_general x8, matrix products, backward_block_step(): jnp.einsum('ghqsk,gqhd->gskhd', score_grad, query_g, preferred_element_ty...  21.4 us
    dot_general x8, matrix products, backward_block_step(): jnp.einsum('gqhd,gskhd->ghqsk', query_g, key_g, preferred_element_type=jn...  18.3 us
  transfers between devices with their start and end apart: 8, of which 5 were waited for; matrix products, arithmetic and copies ran while one was open for 54% of the time, Pallas kernels for 0%

commit v1 on v0

--- a/solution.py
+++ b/solution.py
@@ -7,6 +7,29 @@
 BLK = 128
 MAXB = 8
 EPSILON = 1e-05
+
+
+def split_up(x, dim, devices):
+    dims = x.shape
+    blocks = x.reshape(*dims[:dim], devices, dims[dim] // devices, *dims[dim + 1 :])
+    return jnp.moveaxis(blocks, dim, 0)
+
+
+def in_order(tiles, dim):
+    shape = list(tiles.shape[1:])
+    shape[dim] *= tiles.shape[0]
+    return jnp.moveaxis(tiles, 0, dim).reshape(shape)
+
+
+def pairwise_exchange(x, axis, split_dim, concat_dim):
+    size, position = (lax.axis_size(axis), lax.axis_index(axis))
+    parts = split_up(x, split_dim, size)
+    outs = [parts[position]]
+    for turn in range(1, size):
+        sent = parts[position ^ turn]
+        outs.append(lax.ppermute(sent, axis, [(i, i ^ turn) for i in range(size)]))
+    parts = jnp.stack(outs)[position ^ jnp.arange(size)]
+    return in_order(parts, concat_dim)
 
 
 def layer_norm(feats, gain):
@@ -192,7 +215,7 @@
         head_count,
     )
     query_back, key_back, value_back = (
-        lax.all_to_all(query_grad, "seq", split_axis=0, concat_axis=1, tiled=True),
+        pairwise_exchange(query_grad, "seq", 0, 1),
         lax.all_to_all(key_grad, "seq", split_axis=0, concat_axis=1, tiled=True),
         lax.all_to_all(value_grad, "seq", split_axis=0, concat_axis=1, tiled=True),
     )

time: 637 us -> 614 us (0.964)
  matrix products: 231 us -> 202 us
  local copies, waits for them, and re-layouts: 138 us -> 147 us
    dot_general x8, matrix products: 48.1 us -> 28.1 us  [backward_block_step(): jnp.einsum('gsc,gskhd->ckhd', selector, key_pairs, precision=lax.Precisio...]
    all_to_all x1, waiting for transfers between devices: 0.01 us -> 13.6 us  [body(): lax.all_to_all(query_rows, 'seq', split_axis=1, concat_axis=0, tiled=True)]
    dot_general x8, matrix products: 21.4 us -> 13 us  [backward_block_step(): jnp.einsum('ghqsk,gqhd->gskhd', score_grad, query_g, preferred_element_ty...]
    all_to_all x1, waiting for transfers between devices: 13.7 us -> 5.52 us  [body(): lax.all_to_all(key_rows, 'seq', split_axis=1, concat_axis=0, tiled=True)]
    all_to_all x1 -> x0, waiting for transfers between devices: 7.6 us -> none  [body(): lax.all_to_all(query_grad, 'seq', split_axis=0, concat_axis=1, tiled=True)]
    ppermute x0 -> x7, starting transfers between devices: none -> 7.46 us  [pairwise_exchange(): outs.append(lax.ppermute(sent, axis, [(i, i ^ turn) for i in range(size)]))]
    unnamed x33 -> x45, local copies, waits for them, and re-layouts: 1.91 us -> 9.36 us
    while x120 -> x88, local copies, waits for them, and re-layouts: 42.8 us -> 41.4 us
  transfers between devices with their start and end apart: 8 -> 14, of which waited for: 5 -> 7; matrix products, arithmetic and copies ran while one was open for 54% -> 40% of each run, Pallas kernels for 0% -> 0%
where the time goes in v1:
time: 614 us; the launch traced here: 607 us
  matrix products  202 us (33%)
  local copies, waits for them, and re-layouts  147 us (24%)
  blocking collectives  130 us (21%)
  waiting for transfers between devices  59.9 us (10%)
  starting transfers between devices  39.6 us (6%)
  other arithmetic  24.7 us (4%)
    psum x1, blocking collectives, body(): lax.psum(jnp.concatenate([contract_rows(normed, grad_mixed), contract_row...  130 us
    while x88, local copies, waits for them, and re-layouts  41.4 us
    dot_general x16, matrix products, select_blocks(): jnp.einsum('gsc,cf->gsf', onehot, table, preferred_element_type=jnp.float32)  37.5 us
    slice x16, local copies, waits for them, and re-layouts, select_blocks(): return (picked[..., :HD], picked[..., HD:])  31.6 us
    dot_general x8, matrix products, backward_block_step(): jnp.einsum('gsc,gskhd->ckhd', selector, value_pairs, precision=lax.Precis...  28.1 us
    dot_general x8, matrix products, backward_block_step(): jnp.einsum('gsc,gskhd->ckhd', selector, key_pairs, precision=lax.Precisio...  28.1 us
    dot_general x8, matrix products, backward_block_step(): jnp.einsum('gqhd,gskhd->ghqsk', query_g, key_g, preferred_element_type=jn...  18.4 us
    dot_general x8, matrix products, forward_block_step(): jnp.einsum('gqhd,gskhd->ghqsk', query_g, key_g, preferred_element_type=jn...  14 us
  transfers between devices with their start and end apart: 14, of which 7 were waited for; matrix products, arithmetic and copies ran while one was open for 40% of the time, Pallas kernels for 0%

profile of v1, /device:TPU:0, one launch (start us, length us, event | category | flops | bytes accessed | tf_op | source)
XLA Modules:
  0.0 606.8 jit_solution(5518983661650186190)
XLA Ops:
  8.1 5.5 all-to-all-start.4
  14.3 6.7 %convolution_convert_fusion.2 = bf16[512,3072]{1,0:T(8,128)(2,1)S(1)} fusion(bf16[1024,3072]{1,0:T(8,128)(2,1)} %param.13, bf16[512,1024]{1,0:T(8,128)(2,1)S(1)} %copy-done.7, f32[1024]{0:T(1024)S(1)} %copy-done.20, f32[512]{0:T(512)S(1)} %add_rsqrt_fusion, f32[512]{0:T(512)S(1)} %broadcast_multiply_fusion.2), kind=kOutput, calls=%fused_computation.71 | convolution fusion | flops 3225419776 | bytes 10493952 | tf_op jit(solution)/shard_map/dot_general | solution.py:183
  23.9 5.8 all-to-all-done.4
  29.7 3.6 all-to-all-start.2
  35.5 13.6 %all-to-all-done.2 = bf16[512,8,128]{0,2,1:T(8,128)(2,1)S(1)} async-done(((bf16[512,8,128]{0,2,1:T(8,128)(2,1)}), bf16[512,8,128]{0,2,1:T(8,128)(2,1)S(1)}, u32[]{:S(2)}, u32[]{:S(2)}) %all-to-all-start.2) | async-done | bytes 1048608 | tf_op jit(solution)/shard_map/all_to_all | solution.py:188
  49.1 4.2 all-to-all-start.1
  55.7 13.7 %all-to-all-done.1 = bf16[512,8,128]{0,2,1:T(8,128)(2,1)} async-done(((bf16[512,8,128]{0,2,1:T(8,128)(2,1)}), bf16[512,8,128]{0,2,1:T(8,128)(2,1)}, u32[]{:S(2)}, u32[]{:S(2)}) %all-to-all-start.1) | async-done | bytes 1048608 | tf_op jit(solution)/shard_map/all_to_all | solution.py:190
  69.3 4.8 all-to-all-start
  84.5 5.5 all-to-all-done
  96.4 4.8 copy.69
  101.1 4.5 reshape.191
  106.0 59.6 %while.28 = (s32[]{:T(128)}, bf16[8,4,128,2,64]{2,1,4,3,0:T(4,128)(2,1)S(1)}, f32[8,4,2,128]{3,2,1,0:T(2,128)S(1)}, s32[8,4,8]{2,1,0:T(4,128)S(1)}, bf16[32,3276...) while((s32[]{:T(128)}, ...), condition=%wide.region_5.6_spmd.clone, body=%wide.region_2.5_spmd.clone.sunk | while | flops 348192800 | bytes 23626400 | solution.py:98
  168.8 4.3 all-to-all-start.3
  174.4 209.4 %while.29 = (s32[]{:T(128)}, f32[32,128,2,64]{1,0,3,2:T(8,128)}, f32[32,128,2,64]{1,0,3,2:T(8,128)}, bf16[8,4,128,2,64]{2,1,4,3,0:T(4,128)(2,1)}, s32[8,4,8]{2,1...) while((s32[]{:T(128)}, f32[32,128,2,64]{1,0,3,2:T(8,128)}, ...), condition=%wide.region_8.9_spmd.clone, body=%wide.region_7.8_spmd.clone.sunk | while | flops 1153502208 | bytes 81953840 | solution.py:165
  189.9 3.5 bitcast_add_fusion.5
  216.1 3.5 bitcast_add_fusion.5
  242.2 3.5 bitcast_add_fusion.5
  268.3 3.5 bitcast_add_fusion.5
  294.5 3.5 bitcast_add_fusion.5
  320.6 3.5 bitcast_add_fusion.5
  346.7 3.5 bitcast_add_fusion.5
  372.8 3.5 bitcast_add_fusion.5
  404.9 3.9 collective-permute-done.1
  408.7 5.6 all-to-all-start.5
  418.1 12.3 %all-to-all-done.5 = bf16[8,512,128]{1,2,0:T(8,128)(2,1)} async-done(((bf16[8,512,128]{1,2,0:T(8,128)(2,1)}), bf16[8,512,128]{1,2,0:T(8,128)(2,1)}, u32[]{:S(2)}, u32[]{:S(2)}) %all-to-all-start.5) | async-done | bytes 1048608 | tf_op jit(solution)/shard_map/all_to_all | solution.py:219
  430.4 4.2 all-to-all-start.6
  437.1 4.8 fusion.77
  445.5 5.1 all-to-all-done.6
  450.6 9.0 %multiply_reduce_fusion.1 = (f32[512]{0:T(512)S(1)}, f32[512]{0:T(512)S(1)}, f32[512,1024]{1,0:T(8,128)}) fusion(f32[1024]{0:T(1024)S(1)} %copy-done.21, f32[512]{0:T(512)S(1)} %copy-done.18, f32[512]{0:T(512)S(1)} %copy-done.16, bf16[512,1024]{1,0:T(8,128)(2,1)S(1)} %copy-done.8, bf16[1024,3072]{1,0:T(8,128)(2,1)} %param.13, ...), kind=kOutput, calls=%fused_computation.92 | convolution fusion | flops 3234331648 | bytes 12595200 | tf_op jit(solution)/shard_map/dot_general | solution.py:223
  459.6 5.5 fusion.67
  465.1 6.0 pad_maximum_fusion
  471.1 130.3 %all-reduce.1 = bf16[1024,4096]{1,0:T(8,128)(2,1)} all-reduce(f32[1024,4096]{1,0:T(8,128)} %pad_maximum_fusion), channel_id=1, replica_groups=mesh['dp'=16,'seq'=8] {'dp','seq'}, use_global_device_ids=true, to_apply=%region_11.12 | all-reduce | flops 4194304 | bytes 25165824 | tf_op jit(solution)/shard_map/psum | solution.py:232
  (399 shorter events, 312.0 us)
Async XLA Ops:
  5.7 7.9 %copy-start.7 = (bf16[512,1024]{1,0:T(8,128)(2,1)S(1)}, bf16[512,1024]{1,0:T(8,128)(2,1)}, u32[]{:S(2)}) copy-start(bf16[512,1024]{1,0:T(8,128)(2,1)} %param.11) | copy-start | bytes 3145732
  8.1 6.2 %copy-start.20 = (f32[1024]{0:T(1024)S(1)}, f32[1024]{0:T(1024)}, u32[]{:S(2)}) copy-start(f32[1024]{0:T(1024)} %param.12) | copy-start | bytes 12292
  8.1 21.6 %all-to-all-start.4 = ((bf16[512,8,128]{0,2,1:T(8,128)(2,1)}), bf16[512,8,128]{0,2,1:T(8,128)(2,1)}, u32[]{:S(2)}, u32[]{:S(2)}) async-start(bf16[512,8,128]{0,2,1:T(8,128)(2,1)} %bitcast.237), calls=%async_computation.4 | async-start | bytes 2097152 | tf_op jit(solution)/shard_map/all_to_all | solution.py:205
  13.8 7.1 %copy-start.15 = (f32[512]{0:T(512)}, f32[512]{0:T(512)S(1)}, u32[]{:S(2)}) copy-start(f32[512]{0:T(512)S(1)} %broadcast_multiply_fusion.2) | copy-start | bytes 6148
  14.3 6.7 %copy-start.17 = (f32[512]{0:T(512)}, f32[512]{0:T(512)S(1)}, u32[]{:S(2)}) copy-start(f32[512]{0:T(512)S(1)} %add_rsqrt_fusion) | copy-start | bytes 6148
  29.7 19.4 %all-to-all-start.2 = ((bf16[512,8,128]{0,2,1:T(8,128)(2,1)}), bf16[512,8,128]{0,2,1:T(8,128)(2,1)S(1)}, u32[]{:S(2)}, u32[]{:S(2)}) async-start(bf16[512,8,128]{0,2,1:T(8,128)(2,1)} %bitcast.239), calls=%async_computation.2 | async-start | bytes 2097152 | tf_op jit(solution)/shard_map/all_to_all | solution.py:188
  49.1 20.2 %all-to-all-start.1 = ((bf16[512,8,128]{0,2,1:T(8,128)(2,1)}), bf16[512,8,128]{0,2,1:T(8,128)(2,1)}, u32[]{:S(2)}, u32[]{:S(2)}) async-start(bf16[512,8,128]{0,2,1:T(8,128)(2,1)} %bitcast.238), calls=%async_computation.1 | async-start | bytes 2097152 | tf_op jit(solution)/shard_map/all_to_all | solution.py:190
  53.4 21.3 %copy-start.22 = (s32[1,32]{1,0:T(1,128)S(1)}, s32[1,32]{1,0:T(1,128)}, u32[]{:S(2)}) copy-start(s32[1,32]{1,0:T(1,128)} %param.16) | copy-start | bytes 388
  53.4 22.0 %copy-start.19 = (s32[1,32,8]{1,2,0:T(8,128)S(1)}, s32[1,32,8]{1,2,0:T(8,128)}, u32[]{:S(2)}) copy-start(s32[1,32,8]{1,2,0:T(8,128)} %param.15) | copy-start | bytes 3076
  69.3 20.7 %all-to-all-start = ((bf16[512,8,128]{0,2,1:T(8,128)(2,1)}), bf16[512,8,128]{0,2,1:T(8,128)(2,1)}, u32[]{:S(2)}, u32[]{:S(2)}) async-start(bf16[512,8,128]{0,2,1:T(8,128)(2,1)} %bitcast.236), calls=%async_computation | async-start | bytes 2097152 | tf_op jit(solution)/shard_map/all_to_all | solution.py:189
  168.8 240.0 %all-to-all-start.3 = ((bf16[8,512,128]{1,2,0:T(8,128)(2,1)}), bf16[8,512,128]{1,2,0:T(8,128)(2,1)}, u32[]{:S(2)}, u32[]{:S(2)}) async-start(bf16[8,512,128]{1,2,0:T(8,128)(2,1)} %all_to_all.95), calls=%async_computation.3 | async-start | bytes 2097152 | tf_op jit(solution)/shard_map/all_to_all | solution.py:198
  193.4 2.4 copy-start.4
  386.2 17.0 %collective-permute-start = (bf16[512,128]{0,1:T(8,128)(2,1)}, bf16[512,128]{0,1:T(8,128)(2,1)}, u32[]{:S(2)}, u32[]{:S(2)}) collective-permute-start(bf16[512,128]{0,1:T(8,128)(2,1)} %get-tuple-element.279), channel_id=1, source_target_pairs={{0,1},{1,0},{2,3},{3,2},{4,5},{5,4},{6,7},{7,6},{8,9},{9,8},{10,11... | collective-permute-start | bytes 393224 | tf_op jit(solution)/shard_map/ppermute | solution.py:30
  386.6 48.1 %collective-permute-start.6 = (bf16[512,128]{0,1:T(8,128)(2,1)S(1)}, bf16[512,128]{0,1:T(8,128)(2,1)}, u32[]{:S(2)}, u32[]{:S(2)}) collective-permute-start(bf16[512,128]{0,1:T(8,128)(2,1)S(1)} %get-tuple-element.273), channel_id=1, source_target_pairs={{0,7},{1,6},{2,5},{3,4},{4,3},{5,2},{6,1},{7,0},{8,15},{9,14},{10,... | collective-permute-start | bytes 393224 | tf_op jit(solution)/shard_map/ppermute | solution.py:30
  389.5 27.6 %collective-permute-start.5 = (bf16[512,128]{0,1:T(8,128)(2,1)S(1)}, bf16[512,128]{0,1:T(8,128)(2,1)}, u32[]{:S(2)}, u32[]{:S(2)}) collective-permute-start(bf16[512,128]{0,1:T(8,128)(2,1)S(1)} %get-tuple-element.274), channel_id=1, source_target_pairs={{0,6},{1,7},{2,4},{3,5},{4,2},{5,3},{6,0},{7,1},{8,14},{9,15},{10,... | collective-permute-start | bytes 393224 | tf_op jit(solution)/shard_map/ppermute | solution.py:30
  389.6 26.5 %collective-permute-start.4 = (bf16[512,128]{0,1:T(8,128)(2,1)S(1)}, bf16[512,128]{0,1:T(8,128)(2,1)}, u32[]{:S(2)}, u32[]{:S(2)}) collective-permute-start(bf16[512,128]{0,1:T(8,128)(2,1)S(1)} %get-tuple-element.275), channel_id=1, source_target_pairs={{0,5},{1,4},{2,7},{3,6},{4,1},{5,0},{6,3},{7,2},{8,13},{9,12},{10,... | collective-permute-start | bytes 393224 | tf_op jit(solution)/shard_map/ppermute | solution.py:30
  391.3 24.0 %collective-permute-start.3 = (bf16[512,128]{0,1:T(8,128)(2,1)}, bf16[512,128]{0,1:T(8,128)(2,1)}, u32[]{:S(2)}, u32[]{:S(2)}) collective-permute-start(bf16[512,128]{0,1:T(8,128)(2,1)} %get-tuple-element.276), channel_id=1, source_target_pairs={{0,4},{1,5},{2,6},{3,7},{4,0},{5,1},{6,2},{7,3},{8,12},{9,13},{10,... | collective-permute-start | bytes 393224 | tf_op jit(solution)/shard_map/ppermute | solution.py:30
  396.1 2.7 copy-start.3
  400.5 2.6 copy-start.14
  400.5 3.4 copy-start.11
  403.1 5.6 collective-permute-start.1
  408.7 5.6 collective-permute-start.2
  408.7 21.6 %all-to-all-start.5 = ((bf16[8,512,128]{1,2,0:T(8,128)(2,1)}), bf16[8,512,128]{1,2,0:T(8,128)(2,1)}, u32[]{:S(2)}, u32[]{:S(2)}) async-start(bf16[8,512,128]{1,2,0:T(8,128)(2,1)} %copy.79), calls=%async_computation.5 | async-start | bytes 2097152 | tf_op jit(solution)/shard_map/all_to_all | solution.py:219
  430.4 20.2 %all-to-all-start.6 = ((bf16[8,512,128]{1,2,0:T(8,128)(2,1)}), bf16[8,512,128]{1,2,0:T(8,128)(2,1)}, u32[]{:S(2)}, u32[]{:S(2)}) async-start(bf16[8,512,128]{1,2,0:T(8,128)(2,1)} %copy.80), calls=%async_computation.6 | async-start | bytes 2097152 | tf_op jit(solution)/shard_map/all_to_all | solution.py:220
  437.1 4.8 copy-start.8
  442.0 8.6 %copy-start.16 = (f32[512]{0:T(512)S(1)}, f32[512]{0:T(512)}, u32[]{:S(2)}) copy-start(f32[512]{0:T(512)} %copy-done.15) | copy-start | bytes 6148
  442.0 8.6 %copy-start.18 = (f32[512]{0:T(512)S(1)}, f32[512]{0:T(512)}, u32[]{:S(2)}) copy-start(f32[512]{0:T(512)} %copy-done.17) | copy-start | bytes 6148
  442.0 8.6 %copy-start.21 = (f32[1024]{0:T(1024)S(1)}, f32[1024]{0:T(1024)}, u32[]{:S(2)}) copy-start(f32[1024]{0:T(1024)} %param.12) | copy-start | bytes 12292
  450.6 9.0 %copy-start.12 = (bf16[8,512,128]{1,2,0:T(8,128)(2,1)S(1)}, bf16[8,512,128]{1,2,0:T(8,128)(2,1)}, u32[]{:S(2)}) copy-start(bf16[8,512,128]{1,2,0:T(8,128)(2,1)} %gather_fusion) | copy-start | bytes 3145732
  459.6 5.5 copy-start.9
  601.4 3.1 copy-start.10
  601.4 3.1 copy-start.13
  (40 other events, 73.8 us)
